TPU v7x, 512 devices: a whole 4x8x8 slice. The times are simulated.
512 devices in a mesh: resp: 32 (over x, y), mp: 16 (over z, core).
Axes of the slice: x: 4, y: 8, z: 8, core: 2. Of those that a mesh axis runs over, the one named last changes fastest.
Arguments:
- queries: bfloat16 [32, 512, 4096], P('resp', None, 'mp'), may hold values from -160 to 160
- keys: bfloat16 [32, 512, 512], P('resp'), may hold values from -8 to 8
- values: bfloat16 [32, 512, 512], P('resp'), may hold values from -6 to 6
- out_weight: bfloat16 [4096, 8192], P(None, 'mp'), may hold values from -1.5 to 1.5
- order_bias: float32 [2, 32], replicated, may hold values from -2 to 2
- partners: int32 [32, 6], P('resp'), may hold values from -1 to 31, as said below
- count: int32 [32], P('resp'), may hold values from 1 to 6, as said below
- order: int32 [32, 6], P('resp'), may hold values 0 or 1
Outputs:
- judged: bfloat16 [32, 512, 8192], P('resp', None, 'mp')
Inputs may be any that keep to these rules, and one draw needn't show every extreme that they name: `partners`: slot s of response r is used iff s < count[r]; unused slots hold -1; a used entry names a response other than r at cyclic distance at most 3; the used entries of a row are distinct. `count`: some response has 6 partners and some other has 1.
All inputs are finite; a program needn't handle non-finite values. No bound on the sum of `order` on one device may be relied on, other than what follows from the above.
Results may differ from a plain program's by a relative error of at most 0.0057.
Values may be sent and summed in bfloat16 or wider, within the bound.
A program may use at most 64 MiB of HBM per device.

v0:
```python
import math
import jax
import jax.numpy as jnp
from jax import lax
from jax.sharding import PartitionSpec as P

HQ = 32
KVH = 4
HD = 128
REACH = 3
SLOTS = 6


def shifted(value, axis, steps):
    count = lax.axis_size(axis)
    pairs = [(source, (source + steps) % count) for source in range(count)]
    return lax.ppermute(value, axis, pairs)


def on_device(queries, keys, values, out_weight, order_bias, partners, count, order):
    seq_len = queries.shape[1]
    heads_dev = queries.shape[2] // HD
    group_size = HQ // KVH
    score_scale = 1.0 / math.sqrt(HD)
    first_head = lax.axis_index("mp") * heads_dev
    kv_head = first_head // group_size
    own_keys = lax.dynamic_slice_in_dim(keys[0], kv_head * HD, HD, 1)
    own_values = lax.dynamic_slice_in_dim(values[0], kv_head * HD, HD, 1)
    packed = jnp.stack([own_keys, own_values])
    slot_ids = jnp.arange(SLOTS, dtype=jnp.int32)
    in_use = slot_ids < count[0]
    resp_total = lax.axis_size("resp")
    resp_self = lax.axis_index("resp")
    near_offsets = list(range(1, REACH + 1)) + [-hop_id for hop_id in range(1, REACH + 1)]
    neighbours = []
    for offset in near_offsets:
        neighbours.append(shifted(packed, "resp", -offset))
    stacked = jnp.stack(neighbours)
    distance = (partners[0] - resp_self) % resp_total
    signed = jnp.where(distance <= REACH, distance, distance - resp_total)
    match = (signed[:, None] == jnp.array(near_offsets, jnp.int32)[None, :]) & in_use[:, None]
    flat = stacked.reshape(len(near_offsets), -1)
    picked = jnp.dot(match.astype(jnp.bfloat16), flat, preferred_element_type=jnp.float32)
    picked = picked.astype(jnp.bfloat16).reshape((SLOTS,) + packed.shape)
    key_rows = jnp.concatenate([own_keys[None], picked[:, 0]], 0)
    value_rows = jnp.concatenate([own_values[None], picked[:, 1]], 0)
    query_rows = queries[0].reshape(seq_len, heads_dev, HD)
    scores = (
        jnp.einsum("ihd,sjd->hisj", query_rows, key_rows, preferred_element_type=jnp.float32)
        * score_scale
    )
    bias_dev = lax.dynamic_slice_in_dim(order_bias, first_head, heads_dev, 1)
    slot_bias = jnp.where(order[0][:, None] == 1, bias_dev[1][None, :], bias_dev[0][None, :])
    bias_all = jnp.concatenate([jnp.zeros((1, heads_dev), jnp.float32), slot_bias], 0).T
    scores = scores + bias_all[:, None, :, None]
    causal = jnp.arange(seq_len)[:, None] >= jnp.arange(seq_len)[None, :]
    partner_seen = jnp.broadcast_to(in_use[None, :, None], (seq_len, SLOTS, seq_len))
    visible = jnp.concatenate([causal[:, None, :], partner_seen], 1)
    scores = jnp.where(visible[None], scores, -jnp.inf)
    highest = jnp.max(scores, axis=(2, 3), keepdims=True)
    expo = jnp.exp(scores - highest)
    weights = (expo / jnp.sum(expo, axis=(2, 3), keepdims=True)).astype(jnp.bfloat16)
    attended = jnp.einsum("hisj,sjd->ihd", weights, value_rows, preferred_element_type=jnp.float32)
    attended = attended.astype(jnp.bfloat16).reshape(seq_len, heads_dev * HD)
    judged = jnp.dot(
        lax.all_gather(attended, "mp", axis=1, tiled=True),
        out_weight,
        preferred_element_type=jnp.float32,
    )
    return judged.astype(jnp.bfloat16)[None]


def solution(mesh):
    in_specs = (
        P("resp", None, "mp"),
        P("resp", None, None),
        P("resp", None, None),
        P(None, "mp"),
        P(),
        P("resp", None),
        P("resp"),
        P("resp", None),
    )
    out_specs = P("resp", None, "mp")
    return jax.shard_map(
        on_device, mesh=mesh, in_specs=in_specs, out_specs=out_specs, check_vma=False
    )
```

profile of v0, /device:TPU:1, one launch (start us, length us, event | category | flops | bytes accessed | tf_op | source)
XLA Modules:
  0.0 158.9 jit_solution(16830722555122858521)
XLA Ops:
  6.5 0.0 copy-start
  6.5 0.0 copy-start.4
  6.5 0.0 all-gather.2.cloned.1.call-start
  6.5 1.0 constant_dynamic-slice_fusion.1
  7.6 6.1 %collective-permute-start.5 = (bf16[2,512,128]{2,1,0:T(8,128)(2,1)S(1)}, bf16[2,512,128]{2,1,0:T(8,128)(2,1)S(1)}, u32[]{:S(2)}, u32[]{:S(2)}) collective-permute-start(bf16[2,512,128]{2,1,0:T(8,128)(2,1)S(1)} %pad_maximum_fusion), channel_id=1, source_target_pairs={{0,48},{16,64},{32,80},{48,96},{64,112},{80,128},{96,144},{112,160... | collective-permute-start | bytes 786440 | tf_op jit(solution)/shard_map/ppermute | solution.py:17
  13.7 4.5 %collective-permute-start.4 = (bf16[2,512,128]{2,1,0:T(8,128)(2,1)S(1)}, bf16[2,512,128]{2,1,0:T(8,128)(2,1)S(1)}, u32[]{:S(2)}, u32[]{:S(2)}) collective-permute-start(bf16[2,512,128]{2,1,0:T(8,128)(2,1)S(1)} %pad_maximum_fusion), channel_id=1, source_target_pairs={{0,32},{16,48},{32,64},{48,80},{64,96},{80,112},{96,128},{112,144}... | collective-permute-start | bytes 786440 | tf_op jit(solution)/shard_map/ppermute | solution.py:17
  18.2 2.3 %collective-permute-start.3 = (bf16[2,512,128]{2,1,0:T(8,128)(2,1)S(1)}, bf16[2,512,128]{2,1,0:T(8,128)(2,1)S(1)}, u32[]{:S(2)}, u32[]{:S(2)}) collective-permute-start(bf16[2,512,128]{2,1,0:T(8,128)(2,1)S(1)} %pad_maximum_fusion), channel_id=1, source_target_pairs={{0,16},{16,32},{32,48},{48,64},{64,80},{80,96},{96,112},{112,128},... | collective-permute-start | bytes 786440 | tf_op jit(solution)/shard_map/ppermute | solution.py:17
  20.5 5.8 %collective-permute-start.2 = (bf16[2,512,128]{2,1,0:T(8,128)(2,1)S(1)}, bf16[2,512,128]{2,1,0:T(8,128)(2,1)S(1)}, u32[]{:S(2)}, u32[]{:S(2)}) collective-permute-start(bf16[2,512,128]{2,1,0:T(8,128)(2,1)S(1)} %pad_maximum_fusion), channel_id=1, source_target_pairs={{0,464},{16,480},{32,496},{48,0},{64,16},{80,32},{96,48},{112,64},... | collective-permute-start | bytes 786440 | tf_op jit(solution)/shard_map/ppermute | solution.py:17
  26.3 3.2 %collective-permute-start.1 = (bf16[2,512,128]{2,1,0:T(8,128)(2,1)S(1)}, bf16[2,512,128]{2,1,0:T(8,128)(2,1)S(1)}, u32[]{:S(2)}, u32[]{:S(2)}) collective-permute-start(bf16[2,512,128]{2,1,0:T(8,128)(2,1)S(1)} %pad_maximum_fusion), channel_id=1, source_target_pairs={{0,480},{16,496},{32,0},{48,16},{64,32},{80,48},{96,64},{112,80},{... | collective-permute-start | bytes 786440 | tf_op jit(solution)/shard_map/ppermute | solution.py:17
  29.5 0.1 iota_compare_fusion
  30.3 0.0 copy-done
  30.3 0.1 constant_dynamic-slice_fusion
  30.4 0.1 pad.4.clone
  30.4 1.9 %pad_add_fusion = pred[512,7,512]{0,2,1:T(8,128)(4,1)} fusion(pred[512,1,512]{0,2,1:T(8,128)(4,1)S(1)} %iota_compare_fusion, pred[7]{0:T(512)(128)(4,1)S(1)} %pad.4.clone), kind=kLoop, calls=%fused_computation.6 | loop fusion | flops 1835008 | bytes 2097159 | tf_op jit(solution)/shard_map/concatenate | solution.py:58
  32.3 0.7 compare_bitcast_fusion
  33.0 0.1 broadcast_select_fusion
  33.0 0.0 collective-permute-done.5
  33.0 2.6 %collective-permute-start = (bf16[2,512,128]{2,1,0:T(8,128)(2,1)S(1)}, bf16[2,512,128]{2,1,0:T(8,128)(2,1)S(1)}, u32[]{:S(2)}, u32[]{:S(2)}) collective-permute-start(bf16[2,512,128]{2,1,0:T(8,128)(2,1)S(1)} %pad_maximum_fusion), channel_id=1, source_target_pairs={{0,496},{16,0},{32,16},{48,32},{64,48},{80,64},{96,80},{112,96},{1... | collective-permute-start | bytes 786440 | tf_op jit(solution)/shard_map/ppermute | solution.py:17
  35.7 0.8 copy.11
  36.4 1.7 %reshape_squeeze.3 = bf16[512,2,128]{2,1,0:T(2,128)(2,1)} reshape(bf16[1,512,256]{2,1,0:T(8,128)(2,1)} %param.9) | data formatting | bytes 524288 | tf_op jit(solution)/shard_map/reshape;squeeze | solution.py:47
  38.2 0.0 copy-done.4
  38.2 0.1 stack.32
  38.3 5.9 %collective-permute-done.4 = bf16[2,512,128]{2,1,0:T(8,128)(2,1)S(1)} collective-permute-done((bf16[2,512,128]{2,1,0:T(8,128)(2,1)S(1)}, bf16[2,512,128]{2,1,0:T(8,128)(2,1)S(1)}, u32[]{:S(2)}, u32[]{:S(2)}) %collective-permute-start.4) | collective-permute-done | bytes 262176 | tf_op jit(solution)/shard_map/ppermute | solution.py:17
  44.2 0.1 stack.31
  44.3 0.0 copy-start.3
  44.3 7.6 %collective-permute-done.3 = bf16[2,512,128]{2,1,0:T(8,128)(2,1)S(1)} collective-permute-done((bf16[2,512,128]{2,1,0:T(8,128)(2,1)S(1)}, bf16[2,512,128]{2,1,0:T(8,128)(2,1)S(1)}, u32[]{:S(2)}, u32[]{:S(2)}) %collective-permute-start.3) | collective-permute-done | bytes 262176 | tf_op jit(solution)/shard_map/ppermute | solution.py:17
  51.9 0.9 stack.30
  52.8 0.0 collective-permute-done.2
  52.8 0.9 stack.29
  53.7 2.3 %collective-permute-done.1 = bf16[2,512,128]{2,1,0:T(8,128)(2,1)S(1)} collective-permute-done((bf16[2,512,128]{2,1,0:T(8,128)(2,1)S(1)}, bf16[2,512,128]{2,1,0:T(8,128)(2,1)S(1)}, u32[]{:S(2)}, u32[]{:S(2)}) %collective-permute-start.1) | collective-permute-done | bytes 262176 | tf_op jit(solution)/shard_map/ppermute | solution.py:17
  56.0 0.9 stack.28
  56.9 3.4 %collective-permute-done = bf16[2,512,128]{2,1,0:T(8,128)(2,1)S(1)} collective-permute-done((bf16[2,512,128]{2,1,0:T(8,128)(2,1)S(1)}, bf16[2,512,128]{2,1,0:T(8,128)(2,1)S(1)}, u32[]{:S(2)}, u32[]{:S(2)}) %collective-permute-start) | collective-permute-done | bytes 262176 | tf_op jit(solution)/shard_map/ppermute | solution.py:17
  60.3 0.9 stack.27
  61.2 9.1 %stack.33 = bf16[6,131072]{1,0:T(8,128)(2,1)S(1)} concatenate(bf16[1,131072]{1,0:T(2,128)(2,1)} %stack.27, bf16[1,131072]{1,0:T(2,128)(2,1)} %stack.28, bf16[1,131072]{1,0:T(2,128)(2,1)} %stack.29, bf16[1,131072]{1,0:T(2,128)(2,1)} %stack.30, bf16[1,131072]{1,0:T(2,128)(2,1)S(1)} %stack.31, bf16[1,131072]{1,0:T(2,128)(2,1)S(1)} %stack.32), dimensions={0} | concatenate | bytes 3145728 | tf_op jit(solution)/shard_map/stack | solution.py:38
  70.3 0.0 copy-done.3
  70.3 0.8 fusion.3
  71.1 0.0 copy-start.1
  71.1 0.2 copy.21
  71.3 1.0 fusion.23
  72.3 0.3 copy.19
  72.6 0.2 copy-done.1
  72.9 9.6 %fusion.24 = (f32[2,512]{1,0:T(2,128)S(1)}, f32[2,512,7,512]{1,3,0,2:T(8,128)}) fusion(f32[2,7]{0,1:T(8,128)S(1)} %pad_bitcast_fusion, bf16[512,2,128]{2,1,0:T(2,128)(2,1)} %reshape_squeeze.3, bf16[6,512,128]{2,1,0:T(8,128)(2,1)} %get-tuple-element.6, bf16[1,512,128]{2,1,0:T(8,128)(2,1)S(1)} %get-tuple-element.11, pred[512,7,512]{0,2,1:T(8,128)(4,1)S(1)} %copy-done.1), kind=kOutput, calls=%fused_computation.47 | convolution fusion | flops 956038144 | bytes 17698872 | tf_op jit(solution)/shard_map/ihd,sjd->hisj/dot_general | solution.py:49
  82.4 0.0 copy-start.2
  82.4 7.1 %fusion.1 = f32[2,512]{1,0:T(2,128)S(1)} fusion(f32[2,512,7,512]{1,3,0,2:T(8,128)} %get-tuple-element.10, f32[2,512]{1,0:T(2,128)S(1)} %get-tuple-element.9), kind=kLoop, calls=%fused_computation.5 | loop fusion | flops 7339008 | bytes 14688256 | tf_op jit(solution)/shard_map/reduce_sum | solution.py:62
  89.6 0.0 copy-done.2
  89.6 7.4 %fusion.6 = bf16[128,2,512]{2,0,1:T(8,128)(2,1)} fusion(f32[2,512,7,512]{1,3,0,2:T(8,128)} %get-tuple-element.10, f32[2,512]{1,0:T(2,128)S(1)} %fusion.1, f32[2,512]{1,0:T(2,128)S(1)} %get-tuple-element.9, bf16[6,512,128]{1,2,0:T(8,128)(2,1)S(1)} %bitcast.58, bf16[1,512,128]{1,2,0:T(8,128)(2,1)S(1)} %copy-done.2), kind=kOutput, calls=%fused_computation.12 | convolution fusion | flops 952500224 | bytes 15867904 | tf_op jit(solution)/shard_map/hisj,sjd->ihd/dot_general | solution.py:63
  97.0 0.0 all-gather.2.cloned.1.call-update
  97.0 48.4 %all-gather.2.cloned.1.call-done = bf16[512,4096]{0,1:T(8,128)(2,1)} async-done(((bf16[512,256]{0,1:T(8,128)(2,1)}), bf16[512,4096]{0,1:T(8,128)(2,1)}) %all-gather.2.cloned.1.call-update) | async-done | bytes 4194320 | tf_op jit(solution)/shard_map/all_gather | solution.py:66
  145.4 6.6 %fusion.4 = bf16[1,512,512]{2,1,0:T(8,128)(2,1)} fusion(bf16[512,4096]{0,1:T(8,128)(2,1)} %all-gather.2.cloned.1.call-done, bf16[4096,512]{1,0:T(8,128)(2,1)} %param.12), kind=kOutput, calls=%fused_computation.10 | convolution fusion | flops 2147745792 | bytes 8912896 | tf_op jit(solution)/shard_map/dot_general | solution.py:65
  (5 shorter events, 0.1 us)
Async XLA Ops:
  6.5 23.7 %copy-start = (f32[2,32]{1,0:T(2,128)S(1)}, f32[2,32]{1,0:T(2,128)}, u32[]{:S(2)}) copy-start(f32[2,32]{1,0:T(2,128)} %param.13) | copy-start | bytes 772
  6.5 31.6 %copy-start.4 = (s32[1,6]{1,0:T(1,128)S(1)}, s32[1,6]{1,0:T(1,128)}, u32[]{:S(2)}) copy-start(s32[1,6]{1,0:T(1,128)} %param.14) | copy-start | bytes 76
  6.5 138.9 %all-gather.2.cloned.1.call-start = ((), (), s32[]{:S(2)}) async-start(), calls=%async_computation | async-start | bytes 4456448 | tf_op jit(solution)/shard_map/all_gather | solution.py:66
  7.6 25.5 %collective-permute-start.5 = (bf16[2,512,128]{2,1,0:T(8,128)(2,1)S(1)}, bf16[2,512,128]{2,1,0:T(8,128)(2,1)S(1)}, u32[]{:S(2)}, u32[]{:S(2)}) collective-permute-start(bf16[2,512,128]{2,1,0:T(8,128)(2,1)S(1)} %pad_maximum_fusion), channel_id=1, source_target_pairs={{0,48},{16,64},{32,80},{48,96},{64,112},{80,128},{96,144},{112,160... | collective-permute-start | bytes 786440 | tf_op jit(solution)/shard_map/ppermute | solution.py:17
  13.7 30.5 %collective-permute-start.4 = (bf16[2,512,128]{2,1,0:T(8,128)(2,1)S(1)}, bf16[2,512,128]{2,1,0:T(8,128)(2,1)S(1)}, u32[]{:S(2)}, u32[]{:S(2)}) collective-permute-start(bf16[2,512,128]{2,1,0:T(8,128)(2,1)S(1)} %pad_maximum_fusion), channel_id=1, source_target_pairs={{0,32},{16,48},{32,64},{48,80},{64,96},{80,112},{96,128},{112,144}... | collective-permute-start | bytes 786440 | tf_op jit(solution)/shard_map/ppermute | solution.py:17
  18.2 33.7 %collective-permute-start.3 = (bf16[2,512,128]{2,1,0:T(8,128)(2,1)S(1)}, bf16[2,512,128]{2,1,0:T(8,128)(2,1)S(1)}, u32[]{:S(2)}, u32[]{:S(2)}) collective-permute-start(bf16[2,512,128]{2,1,0:T(8,128)(2,1)S(1)} %pad_maximum_fusion), channel_id=1, source_target_pairs={{0,16},{16,32},{32,48},{48,64},{64,80},{80,96},{96,112},{112,128},... | collective-permute-start | bytes 786440 | tf_op jit(solution)/shard_map/ppermute | solution.py:17
  20.5 32.3 %collective-permute-start.2 = (bf16[2,512,128]{2,1,0:T(8,128)(2,1)S(1)}, bf16[2,512,128]{2,1,0:T(8,128)(2,1)S(1)}, u32[]{:S(2)}, u32[]{:S(2)}) collective-permute-start(bf16[2,512,128]{2,1,0:T(8,128)(2,1)S(1)} %pad_maximum_fusion), channel_id=1, source_target_pairs={{0,464},{16,480},{32,496},{48,0},{64,16},{80,32},{96,48},{112,64},... | collective-permute-start | bytes 786440 | tf_op jit(solution)/shard_map/ppermute | solution.py:17
  26.3 29.7 %collective-permute-start.1 = (bf16[2,512,128]{2,1,0:T(8,128)(2,1)S(1)}, bf16[2,512,128]{2,1,0:T(8,128)(2,1)S(1)}, u32[]{:S(2)}, u32[]{:S(2)}) collective-permute-start(bf16[2,512,128]{2,1,0:T(8,128)(2,1)S(1)} %pad_maximum_fusion), channel_id=1, source_target_pairs={{0,480},{16,496},{32,0},{48,16},{64,32},{80,48},{96,64},{112,80},{... | collective-permute-start | bytes 786440 | tf_op jit(solution)/shard_map/ppermute | solution.py:17
  33.0 27.3 %collective-permute-start = (bf16[2,512,128]{2,1,0:T(8,128)(2,1)S(1)}, bf16[2,512,128]{2,1,0:T(8,128)(2,1)S(1)}, u32[]{:S(2)}, u32[]{:S(2)}) collective-permute-start(bf16[2,512,128]{2,1,0:T(8,128)(2,1)S(1)} %pad_maximum_fusion), channel_id=1, source_target_pairs={{0,496},{16,0},{32,16},{48,32},{64,48},{80,64},{96,80},{112,96},{1... | collective-permute-start | bytes 786440 | tf_op jit(solution)/shard_map/ppermute | solution.py:17
  44.3 26.0 %copy-start.3 = (s32[6]{0:T(128)S(1)}, s32[6]{0:T(128)}, u32[]{:S(2)}) copy-start(s32[6]{0:T(128)} %constant.62.clone) | copy-start | bytes 76
  71.1 1.8 %copy-start.1 = (pred[512,7,512]{0,2,1:T(8,128)(4,1)S(1)}, pred[512,7,512]{0,2,1:T(8,128)(4,1)}, u32[]{:S(2)}) copy-start(pred[512,7,512]{0,2,1:T(8,128)(4,1)} %pad_add_fusion) | copy-start | bytes 5505028
  82.4 7.1 %copy-start.2 = (bf16[1,512,128]{1,2,0:T(8,128)(2,1)S(1)}, bf16[1,512,128]{1,2,0:T(8,128)(2,1)}, u32[]{:S(2)}) copy-start(bf16[1,512,128]{1,2,0:T(8,128)(2,1)} %copy.11) | copy-start | bytes 393220
Sparse Core Ops, SparseCore 0:
  97.1 48.2 all-gather.1
where the time goes:
time: 160 us; the launch traced here: 159 us
  waiting for transfers between devices  67.6 us (42%)
  starting transfers between devices  24.5 us (15%)
  matrix products  24.4 us (15%)
  local copies, waits for them, and re-layouts  18.3 us (11%)
  between operations  14.2 us (9%)
  other arithmetic  9.86 us (6%)
    all_gather x1, waiting for transfers between devices, on_device(): lax.all_gather(attended, 'mp', axis=1, tiled=True)  48.4 us
    ppermute x6, starting transfers between devices, shifted(): return lax.ppermute(value, axis, pairs)  24.5 us
    ppermute x6, waiting for transfers between devices, shifted(): return lax.ppermute(value, axis, pairs)  19.2 us
    another operation x7, local copies, waits for them, and re-layouts, on_device(): stacked = jnp.stack(neighbours)  12.9 us
    dot_general x1, matrix products, on_device(): jnp.einsum('ihd,sjd->hisj', query_rows, key_rows, preferred_element_type=...  9.58 us
    dot_general x1, matrix products, on_device(): jnp.einsum('hisj,sjd->ihd', weights, value_rows, preferred_element_type=j...  7.41 us
    reduce_sum x1, other arithmetic, on_device(): jnp.sum(expo, axis=(2, 3), keepdims=True)  7.14 us
    dot_general x1, matrix products, on_device(): jnp.dot(lax.all_gather(attended, 'mp', axis=1, tiled=True), out_weight, p...  6.61 us
  transfers between devices with their start and end apart: 7, of which 5 were waited for; matrix products, arithmetic and copies ran while one was open for 5% of the time, Pallas kernels for 0%

commit v1 on v0

--- a/solution.py
+++ b/solution.py
@@ -63,7 +63,9 @@
     attended = jnp.einsum("hisj,sjd->ihd", weights, value_rows, preferred_element_type=jnp.float32)
     attended = attended.astype(jnp.bfloat16).reshape(seq_len, heads_dev * HD)
     judged = jnp.dot(
-        lax.all_gather(attended, "mp", axis=1, tiled=True),
+        jnp.concatenate(
+            lax.all_to_all(jnp.stack([attended] * lax.axis_size("mp")), "mp", 0, 0), axis=1
+        ),
         out_weight,
         preferred_element_type=jnp.float32,
     )

time: 160 us -> 203 us (1.27)
  blocking collectives: 0 us -> 109 us
  waiting for transfers between devices: 67.6 us -> 19.2 us
  between operations: 14.2 us -> 0.85 us
  matrix products: 24.4 us -> 20.2 us
    all_to_all x0 -> x1, blocking collectives: none -> 109 us  [on_device(): lax.all_to_all(jnp.stack([attended] * lax.axis_size('mp')), 'mp', 0, 0)]
    all_gather x1 -> x0, waiting for transfers between devices: 48.4 us -> none  [on_device(): lax.all_gather(attended, 'mp', axis=1, tiled=True)]
    dot_general x1, matrix products: 6.61 us -> 3.15 us  [on_device(): jnp.dot(jnp.concatenate(lax.all_to_all(jnp.stack([attended] * lax.axis_si...]
  transfers between devices with their start and end apart: 7 -> 6, of which waited for: 5 -> 4; matrix products, arithmetic and copies ran while one was open for 5% -> 4% of each run, Pallas kernels for 0% -> 0%
where the time goes in v1:
time: 203 us; the launch traced here: 202 us
  blocking collectives  109 us (54%)
  starting transfers between devices  24.5 us (12%)
  matrix products  20.2 us (10%)
  waiting for transfers between devices  19.2 us (9%)
  local copies, waits for them, and re-layouts  18.7 us (9%)
  other arithmetic  9.87 us (5%)
    all_to_all x1, blocking collectives, on_device(): lax.all_to_all(jnp.stack([attended] * lax.axis_size('mp')), 'mp', 0, 0)  109 us
    ppermute x6, starting transfers between devices, shifted(): return lax.ppermute(value, axis, pairs)  24.5 us
    ppermute x6, waiting for transfers between devices, shifted(): return lax.ppermute(value, axis, pairs)  19.2 us
    another operation x7, local copies, waits for them, and re-layouts, on_device(): stacked = jnp.stack(neighbours)  12.9 us
    dot_general x1, matrix products, on_device(): jnp.einsum('ihd,sjd->hisj', query_rows, key_rows, preferred_element_type=...  9.59 us
    reduce_sum x1, other arithmetic, on_device(): jnp.sum(expo, axis=(2, 3), keepdims=True)  7.14 us
    dot_general x1, matrix products, on_device(): jnp.einsum('hisj,sjd->ihd', weights, value_rows, preferred_element_type=j...  6.73 us
  transfers between devices with their start and end apart: 6, of which 4 were waited for; matrix products, arithmetic and copies ran while one was open for 4% of the time, Pallas kernels for 0%

profile of v1, /device:TPU:1, one launch (start us, length us, event | category | flops | bytes accessed | tf_op | source)
XLA Modules:
  0.0 202.0 jit_solution(3201608569179286030)
XLA Ops:
  0.0 0.0 copy-start
  0.0 0.0 copy-start.5
  0.0 1.0 constant_dynamic-slice_fusion.1
  1.1 6.1 %collective-permute-start.5 = (bf16[2,512,128]{2,1,0:T(8,128)(2,1)S(1)}, bf16[2,512,128]{2,1,0:T(8,128)(2,1)S(1)}, u32[]{:S(2)}, u32[]{:S(2)}) collective-permute-start(bf16[2,512,128]{2,1,0:T(8,128)(2,1)S(1)} %pad_maximum_fusion), channel_id=1, source_target_pairs={{0,48},{16,64},{32,80},{48,96},{64,112},{80,128},{96,144},{112,160... | collective-permute-start | bytes 786440 | tf_op jit(solution)/shard_map/ppermute | solution.py:17
  7.1 4.5 %collective-permute-start.4 = (bf16[2,512,128]{2,1,0:T(8,128)(2,1)S(1)}, bf16[2,512,128]{2,1,0:T(8,128)(2,1)S(1)}, u32[]{:S(2)}, u32[]{:S(2)}) collective-permute-start(bf16[2,512,128]{2,1,0:T(8,128)(2,1)S(1)} %pad_maximum_fusion), channel_id=1, source_target_pairs={{0,32},{16,48},{32,64},{48,80},{64,96},{80,112},{96,128},{112,144}... | collective-permute-start | bytes 786440 | tf_op jit(solution)/shard_map/ppermute | solution.py:17
  11.7 2.3 %collective-permute-start.3 = (bf16[2,512,128]{2,1,0:T(8,128)(2,1)S(1)}, bf16[2,512,128]{2,1,0:T(8,128)(2,1)S(1)}, u32[]{:S(2)}, u32[]{:S(2)}) collective-permute-start(bf16[2,512,128]{2,1,0:T(8,128)(2,1)S(1)} %pad_maximum_fusion), channel_id=1, source_target_pairs={{0,16},{16,32},{32,48},{48,64},{64,80},{80,96},{96,112},{112,128},... | collective-permute-start | bytes 786440 | tf_op jit(solution)/shard_map/ppermute | solution.py:17
  14.0 5.8 %collective-permute-start.2 = (bf16[2,512,128]{2,1,0:T(8,128)(2,1)S(1)}, bf16[2,512,128]{2,1,0:T(8,128)(2,1)S(1)}, u32[]{:S(2)}, u32[]{:S(2)}) collective-permute-start(bf16[2,512,128]{2,1,0:T(8,128)(2,1)S(1)} %pad_maximum_fusion), channel_id=1, source_target_pairs={{0,464},{16,480},{32,496},{48,0},{64,16},{80,32},{96,48},{112,64},... | collective-permute-start | bytes 786440 | tf_op jit(solution)/shard_map/ppermute | solution.py:17
  19.7 3.2 %collective-permute-start.1 = (bf16[2,512,128]{2,1,0:T(8,128)(2,1)S(1)}, bf16[2,512,128]{2,1,0:T(8,128)(2,1)S(1)}, u32[]{:S(2)}, u32[]{:S(2)}) collective-permute-start(bf16[2,512,128]{2,1,0:T(8,128)(2,1)S(1)} %pad_maximum_fusion), channel_id=1, source_target_pairs={{0,480},{16,496},{32,0},{48,16},{64,32},{80,48},{96,64},{112,80},{... | collective-permute-start | bytes 786440 | tf_op jit(solution)/shard_map/ppermute | solution.py:17
  23.0 0.1 iota_compare_fusion
  23.7 0.0 copy-done
  23.8 0.1 constant_dynamic-slice_fusion
  23.8 0.1 pad.4.clone
  23.9 1.9 pad_add_fusion
  25.8 0.7 compare_bitcast_fusion
  26.4 0.1 broadcast_select_fusion
  26.5 0.0 collective-permute-done.5
  26.5 2.6 %collective-permute-start = (bf16[2,512,128]{2,1,0:T(8,128)(2,1)S(1)}, bf16[2,512,128]{2,1,0:T(8,128)(2,1)S(1)}, u32[]{:S(2)}, u32[]{:S(2)}) collective-permute-start(bf16[2,512,128]{2,1,0:T(8,128)(2,1)S(1)} %pad_maximum_fusion), channel_id=1, source_target_pairs={{0,496},{16,0},{32,16},{48,32},{64,48},{80,64},{96,80},{112,96},{1... | collective-permute-start | bytes 786440 | tf_op jit(solution)/shard_map/ppermute | solution.py:17
  29.2 0.8 copy.17
  29.9 1.7 reshape_squeeze.3
  31.6 0.0 copy-done.5
  31.6 0.1 stack.35
  31.7 5.9 %collective-permute-done.4 = bf16[2,512,128]{2,1,0:T(8,128)(2,1)S(1)} collective-permute-done((bf16[2,512,128]{2,1,0:T(8,128)(2,1)S(1)}, bf16[2,512,128]{2,1,0:T(8,128)(2,1)S(1)}, u32[]{:S(2)}, u32[]{:S(2)}) %collective-permute-start.4) | collective-permute-done | bytes 262176 | tf_op jit(solution)/shard_map/ppermute | solution.py:17
  37.7 0.1 stack.34
  37.8 0.0 copy-start.3
  37.8 7.6 %collective-permute-done.3 = bf16[2,512,128]{2,1,0:T(8,128)(2,1)S(1)} collective-permute-done((bf16[2,512,128]{2,1,0:T(8,128)(2,1)S(1)}, bf16[2,512,128]{2,1,0:T(8,128)(2,1)S(1)}, u32[]{:S(2)}, u32[]{:S(2)}) %collective-permute-start.3) | collective-permute-done | bytes 262176 | tf_op jit(solution)/shard_map/ppermute | solution.py:17
  45.4 0.9 stack.33
  46.3 0.0 collective-permute-done.2
  46.3 0.9 stack.32
  47.2 2.3 %collective-permute-done.1 = bf16[2,512,128]{2,1,0:T(8,128)(2,1)S(1)} collective-permute-done((bf16[2,512,128]{2,1,0:T(8,128)(2,1)S(1)}, bf16[2,512,128]{2,1,0:T(8,128)(2,1)S(1)}, u32[]{:S(2)}, u32[]{:S(2)}) %collective-permute-start.1) | collective-permute-done | bytes 262176 | tf_op jit(solution)/shard_map/ppermute | solution.py:17
  49.5 0.9 stack.31
  50.4 3.4 %collective-permute-done = bf16[2,512,128]{2,1,0:T(8,128)(2,1)S(1)} collective-permute-done((bf16[2,512,128]{2,1,0:T(8,128)(2,1)S(1)}, bf16[2,512,128]{2,1,0:T(8,128)(2,1)S(1)}, u32[]{:S(2)}, u32[]{:S(2)}) %collective-permute-start) | collective-permute-done | bytes 262176 | tf_op jit(solution)/shard_map/ppermute | solution.py:17
  53.8 0.9 stack.30
  54.7 9.1 %stack.36 = bf16[6,131072]{1,0:T(8,128)(2,1)S(1)} concatenate(bf16[1,131072]{1,0:T(2,128)(2,1)} %stack.30, bf16[1,131072]{1,0:T(2,128)(2,1)} %stack.31, bf16[1,131072]{1,0:T(2,128)(2,1)} %stack.32, bf16[1,131072]{1,0:T(2,128)(2,1)} %stack.33, bf16[1,131072]{1,0:T(2,128)(2,1)S(1)} %stack.34, bf16[1,131072]{1,0:T(2,128)(2,1)S(1)} %stack.35), dimensions={0} | concatenate | bytes 3145728 | tf_op jit(solution)/shard_map/stack | solution.py:38
  63.8 0.0 copy-done.3
  63.8 0.8 fusion.3
  64.5 0.0 copy-start.1
  64.6 0.2 copy.27
  64.8 1.0 fusion.23
  65.8 0.3 copy.25
  66.1 0.3 copy-done.1
  66.3 9.6 %fusion.24 = (f32[2,512]{1,0:T(2,128)S(1)}, f32[2,512,7,512]{1,3,0,2:T(8,128)}) fusion(f32[2,7]{0,1:T(8,128)S(1)} %pad_bitcast_fusion, bf16[512,2,128]{2,1,0:T(2,128)(2,1)} %reshape_squeeze.3, bf16[6,512,128]{2,1,0:T(8,128)(2,1)} %get-tuple-element.6, bf16[1,512,128]{2,1,0:T(8,128)(2,1)S(1)} %get-tuple-element.11, pred[512,7,512]{0,2,1:T(8,128)(4,1)S(1)} %copy-done.1), kind=kOutput, calls=%fused_computation.47 | convolution fusion | flops 956038144 | bytes 17698872 | tf_op jit(solution)/shard_map/ihd,sjd->hisj/dot_general | solution.py:49
  75.9 0.0 copy-start.2
  75.9 7.1 %fusion.1 = f32[2,512]{1,0:T(2,128)S(1)} fusion(f32[2,512,7,512]{1,3,0,2:T(8,128)} %get-tuple-element.10, f32[2,512]{1,0:T(2,128)S(1)} %get-tuple-element.9), kind=kLoop, calls=%fused_computation.5 | loop fusion | flops 7339008 | bytes 14688256 | tf_op jit(solution)/shard_map/reduce_sum | solution.py:62
  83.1 0.0 copy-done.2
  83.1 6.7 %fusion.6 = bf16[128,2,512]{2,0,1:T(8,128)(2,1)S(1)} fusion(f32[2,512,7,512]{1,3,0,2:T(8,128)} %get-tuple-element.10, f32[2,512]{1,0:T(2,128)S(1)} %fusion.1, f32[2,512]{1,0:T(2,128)S(1)} %get-tuple-element.9, bf16[6,512,128]{1,2,0:T(8,128)(2,1)S(1)} %bitcast.62, bf16[1,512,128]{1,2,0:T(8,128)(2,1)S(1)} %copy-done.2), kind=kOutput, calls=%fused_computation.12 | convolution fusion | flops 952500224 | bytes 15867904 | tf_op jit(solution)/shard_map/hisj,sjd->ihd/dot_general | solution.py:63
  89.8 0.4 stack.37
  90.2 0.0 copy-start.4
  90.2 108.6 %all_to_all.5 = bf16[16,512,256]{1,2,0:T(8,128)(2,1)S(1)} all-to-all(bf16[16,512,256]{1,2,0:T(8,128)(2,1)S(1)} %stack.37), channel_id=1, replica_groups=mesh['resp'=32,'mp'=16] {'mp'}, dimensions={0} | all-to-all | bytes 8388608 | tf_op jit(solution)/shard_map/all_to_all | solution.py:67
  198.9 0.0 copy-done.4
  198.9 3.1 %fusion.4 = bf16[1,512,512]{2,1,0:T(8,128)(2,1)} fusion(bf16[512,4096]{0,1:T(8,128)(2,1)S(1)} %bitcast.61, bf16[4096,512]{1,0:T(8,128)(2,1)S(1)} %copy-done.4), kind=kOutput, calls=%fused_computation.10 | convolution fusion | flops 2147745792 | bytes 8912896 | tf_op jit(solution)/shard_map/dot_general | solution.py:65
  (5 shorter events, 0.1 us)
Async XLA Ops:
  0.0 23.7 %copy-start = (f32[2,32]{1,0:T(2,128)S(1)}, f32[2,32]{1,0:T(2,128)}, u32[]{:S(2)}) copy-start(f32[2,32]{1,0:T(2,128)} %param.13) | copy-start | bytes 772
  0.0 31.6 %copy-start.5 = (s32[1,6]{1,0:T(1,128)S(1)}, s32[1,6]{1,0:T(1,128)}, u32[]{:S(2)}) copy-start(s32[1,6]{1,0:T(1,128)} %param.14) | copy-start | bytes 76
  1.1 25.5 %collective-permute-start.5 = (bf16[2,512,128]{2,1,0:T(8,128)(2,1)S(1)}, bf16[2,512,128]{2,1,0:T(8,128)(2,1)S(1)}, u32[]{:S(2)}, u32[]{:S(2)}) collective-permute-start(bf16[2,512,128]{2,1,0:T(8,128)(2,1)S(1)} %pad_maximum_fusion), channel_id=1, source_target_pairs={{0,48},{16,64},{32,80},{48,96},{64,112},{80,128},{96,144},{112,160... | collective-permute-start | bytes 786440 | tf_op jit(solution)/shard_map/ppermute | solution.py:17
  7.1 30.5 %collective-permute-start.4 = (bf16[2,512,128]{2,1,0:T(8,128)(2,1)S(1)}, bf16[2,512,128]{2,1,0:T(8,128)(2,1)S(1)}, u32[]{:S(2)}, u32[]{:S(2)}) collective-permute-start(bf16[2,512,128]{2,1,0:T(8,128)(2,1)S(1)} %pad_maximum_fusion), channel_id=1, source_target_pairs={{0,32},{16,48},{32,64},{48,80},{64,96},{80,112},{96,128},{112,144}... | collective-permute-start | bytes 786440 | tf_op jit(solution)/shard_map/ppermute | solution.py:17
  11.7 33.7 %collective-permute-start.3 = (bf16[2,512,128]{2,1,0:T(8,128)(2,1)S(1)}, bf16[2,512,128]{2,1,0:T(8,128)(2,1)S(1)}, u32[]{:S(2)}, u32[]{:S(2)}) collective-permute-start(bf16[2,512,128]{2,1,0:T(8,128)(2,1)S(1)} %pad_maximum_fusion), channel_id=1, source_target_pairs={{0,16},{16,32},{32,48},{48,64},{64,80},{80,96},{96,112},{112,128},... | collective-permute-start | bytes 786440 | tf_op jit(solution)/shard_map/ppermute | solution.py:17
  14.0 32.3 %collective-permute-start.2 = (bf16[2,512,128]{2,1,0:T(8,128)(2,1)S(1)}, bf16[2,512,128]{2,1,0:T(8,128)(2,1)S(1)}, u32[]{:S(2)}, u32[]{:S(2)}) collective-permute-start(bf16[2,512,128]{2,1,0:T(8,128)(2,1)S(1)} %pad_maximum_fusion), channel_id=1, source_target_pairs={{0,464},{16,480},{32,496},{48,0},{64,16},{80,32},{96,48},{112,64},... | collective-permute-start | bytes 786440 | tf_op jit(solution)/shard_map/ppermute | solution.py:17
  19.7 29.7 %collective-permute-start.1 = (bf16[2,512,128]{2,1,0:T(8,128)(2,1)S(1)}, bf16[2,512,128]{2,1,0:T(8,128)(2,1)S(1)}, u32[]{:S(2)}, u32[]{:S(2)}) collective-permute-start(bf16[2,512,128]{2,1,0:T(8,128)(2,1)S(1)} %pad_maximum_fusion), channel_id=1, source_target_pairs={{0,480},{16,496},{32,0},{48,16},{64,32},{80,48},{96,64},{112,80},{... | collective-permute-start | bytes 786440 | tf_op jit(solution)/shard_map/ppermute | solution.py:17
  26.5 27.3 %collective-permute-start = (bf16[2,512,128]{2,1,0:T(8,128)(2,1)S(1)}, bf16[2,512,128]{2,1,0:T(8,128)(2,1)S(1)}, u32[]{:S(2)}, u32[]{:S(2)}) collective-permute-start(bf16[2,512,128]{2,1,0:T(8,128)(2,1)S(1)} %pad_maximum_fusion), channel_id=1, source_target_pairs={{0,496},{16,0},{32,16},{48,32},{64,48},{80,64},{96,80},{112,96},{1... | collective-permute-start | bytes 786440 | tf_op jit(solution)/shard_map/ppermute | solution.py:17
  37.8 26.0 %copy-start.3 = (s32[6]{0:T(128)S(1)}, s32[6]{0:T(128)}, u32[]{:S(2)}) copy-start(s32[6]{0:T(128)} %constant.62.clone) | copy-start | bytes 76
  64.5 1.8 copy-start.1
  75.9 7.1 %copy-start.2 = (bf16[1,512,128]{1,2,0:T(8,128)(2,1)S(1)}, bf16[1,512,128]{1,2,0:T(8,128)(2,1)}, u32[]{:S(2)}) copy-start(bf16[1,512,128]{1,2,0:T(8,128)(2,1)} %copy.17) | copy-start | bytes 393220
  90.2 108.7 %copy-start.4 = (bf16[4096,512]{1,0:T(8,128)(2,1)S(1)}, bf16[4096,512]{1,0:T(8,128)(2,1)}, u32[]{:S(2)}) copy-start(bf16[4096,512]{1,0:T(8,128)(2,1)} %param.12) | copy-start | bytes 12582916
